TPU v7x, 32 devices: a whole 2x2x4 slice. The times are simulated.
32 devices in a mesh: layer: 2 (over core), rows: 16 (over z, y, x).
Axes of the slice: x: 2, y: 2, z: 4, core: 2. Of those that a mesh axis runs over, the one named last changes fastest.
Arguments:
- frames: bfloat16 [3, 32, 256, 256], P(None, 'rows'), may hold values from -6 to 6
- initial_state: bfloat16 [2, 32, 256, 256], P('layer', 'rows'), may hold values from -3 to 3
- w_gates: bfloat16 [2, 3, 3, 512, 512], P('layer'), may hold values from -0.25 to 0.25
- w_cand: bfloat16 [2, 3, 3, 512, 256], P('layer'), may hold values from -0.125 to 0.125
- biases: float32 [2, 768], P('layer'), may hold values from -4 to 4
Outputs:
- hidden_frames: bfloat16 [2, 3, 32, 256, 256], P('layer', None, 'rows')
All inputs are finite; a program needn't handle non-finite values.
Results may differ from a plain program's by a relative error of at most 0.0048.
Values may be sent and summed in bfloat16 or wider, within the bound.
A program may use at most 64 MiB of HBM per device.

v0:
```python
import jax
import jax.numpy as jnp
from jax import lax
from jax.sharding import PartitionSpec as P


def with_halo(block, sides, width):
    for axis, dim in sides:
        count = lax.axis_size(axis)
        forward = [(i, i + 1) for i in range(count - 1)]
        backward = [(target, source) for source, target in forward]
        low = lax.ppermute(
            lax.slice_in_dim(block, block.shape[dim] - width, None, axis=dim), axis, forward
        )
        high = lax.ppermute(lax.slice_in_dim(block, 0, width, axis=dim), axis, backward)
        block = jnp.concatenate([low, block, high], axis=dim)
    return block


def shifted(block, axis, distance):
    devices = range(lax.axis_size(axis))
    route = [(i - distance, i) for i in devices if i - distance in devices]
    return lax.ppermute(block, axis, route)


def convolve(padded, weight):
    out_rows = padded.shape[0] - 2
    out_cols = padded.shape[1] - 2
    pieces = [
        padded[row_off : row_off + out_rows, col_off : col_off + out_cols]
        for row_off in range(3)
        for col_off in range(3)
    ]
    stacked = jnp.concatenate(pieces, axis=-1).reshape(out_rows * out_cols, -1)
    weight_flat = weight.reshape(-1, weight.shape[-1])
    return jnp.dot(stacked, weight_flat, preferred_element_type=jnp.float32).reshape(
        out_rows, out_cols, -1
    )


def pad_cols(field, width):
    return jnp.pad(field, ((0, 0), (width, width), (0, 0)))


def gru_step(inputs, hidden, gate_weight, cand_weight, bias_row, widen_one, widen_reset):
    channels = hidden.shape[-1]
    joined = jnp.concatenate([inputs, hidden], -1)
    hidden_f = hidden.astype(jnp.float32)
    padded = widen_one(joined)
    gate_all = jax.nn.sigmoid(convolve(padded, gate_weight) + bias_row[: 2 * channels])
    update = gate_all[..., :channels]
    reset_state = (gate_all[..., channels:] * hidden_f).astype(jnp.bfloat16)
    reset_wide = widen_reset(reset_state)
    cand_in = jnp.concatenate([padded[..., :channels], reset_wide], -1)
    candidate = jnp.tanh(convolve(cand_in, cand_weight) + bias_row[2 * channels :])
    return ((1.0 - update) * hidden_f + update * candidate).astype(jnp.bfloat16)


def shards(frames, initial_state, w_gates, w_cand, biases):
    frame_count = frames.shape[0]

    def strip_one(field):
        return pad_cols(with_halo(field, (("rows", 0),), 1), 1)

    def strip_reset(field):
        return pad_cols(with_halo(field, (("rows", 0),), 1), 1)

    section_index = lax.axis_index("layer")
    gate_weight = w_gates[0]
    cand_weight = w_cand[0]
    bias_row = biases[0]
    hidden = initial_state[0]
    produced = jnp.zeros((frame_count,) + hidden.shape, jnp.bfloat16)
    passed = jnp.zeros_like(hidden)
    for step_index in range(frame_count + 1):
        if step_index > 0:
            received = shifted(passed, "layer", 1)
        else:
            received = jnp.zeros_like(hidden)
        own_frame = frames[min(step_index, frame_count - 1)]
        inputs = jnp.where(section_index == 0, own_frame, received)
        fresh_state = gru_step(
            inputs, hidden, gate_weight, cand_weight, bias_row, strip_one, strip_reset
        )
        active = jnp.logical_or(
            jnp.logical_and(section_index == 0, step_index < frame_count),
            jnp.logical_and(section_index == 1, step_index >= 1),
        )
        hidden = jnp.where(active, fresh_state, hidden)
        slot_index = jnp.clip(step_index - section_index, 0, frame_count - 1)
        current = lax.dynamic_index_in_dim(produced, slot_index, 0, keepdims=False)
        produced = lax.dynamic_update_index_in_dim(
            produced, jnp.where(active, fresh_state, current), slot_index, 0
        )
        passed = fresh_state
    return produced[None]


def solution(mesh):
    placed = (
        P(None, "rows", None, None),
        P("layer", "rows", None, None),
        P("layer", None, None, None, None),
        P("layer", None, None, None, None),
        P("layer", None),
    )
    return jax.shard_map(
        shards,
        mesh=mesh,
        in_specs=placed,
        out_specs=P("layer", None, "rows", None, None),
        check_vma=False,
    )
```

profile of v0, /device:TPU:22, one launch (start us, length us, event | category | flops | bytes accessed | tf_op | source)
XLA Modules:
  0.0 161.2 jit_solution(7234095389509302540)
XLA Ops:
  0.0 1.1 select_bitcast_fusion
  1.2 1.2 fusion.123
  2.3 3.5 %collective-permute-start = (bf16[1,256,512]{2,1,0:T(8,128)(2,1)S(1)}, bf16[1,256,512]{2,1,0:T(8,128)(2,1)S(1)}, u32[]{:S(2)}, u32[]{:S(2)}) collective-permute-start(bf16[1,256,512]{2,1,0:T(8,128)(2,1)S(1)} %get-tuple-element.11), channel_id=1, source_target_pairs={{0,1},{1,2},{2,3},{3,4},{4,5},{5,6},{6,7},{7,8},{8,9},{9,10},{10,1... | collective-permute-start | bytes 786440 | tf_op jit(solution)/shard_map/ppermute | solution.py:12
  5.9 2.4 %collective-permute-start.1 = (bf16[1,256,512]{2,1,0:T(8,128)(2,1)S(1)}, bf16[1,256,512]{2,1,0:T(8,128)(2,1)S(1)}, u32[]{:S(2)}, u32[]{:S(2)}) collective-permute-start(bf16[1,256,512]{2,1,0:T(8,128)(2,1)S(1)} %get-tuple-element.12), channel_id=1, source_target_pairs={{1,0},{2,1},{3,2},{4,3},{5,4},{6,5},{7,6},{8,7},{9,8},{10,9},{11,1... | collective-permute-start | bytes 786440 | tf_op jit(solution)/shard_map/ppermute | solution.py:15
  9.0 4.5 %collective-permute-done = bf16[1,256,512]{2,1,0:T(8,128)(2,1)S(1)} collective-permute-done((bf16[1,256,512]{2,1,0:T(8,128)(2,1)S(1)}, bf16[1,256,512]{2,1,0:T(8,128)(2,1)S(1)}, u32[]{:S(2)}, u32[]{:S(2)}) %collective-permute-start) | collective-permute-done | bytes 262176 | tf_op jit(solution)/shard_map/ppermute | solution.py:12
  13.5 3.9 %collective-permute-done.1 = bf16[1,256,512]{2,1,0:T(8,128)(2,1)S(1)} collective-permute-done((bf16[1,256,512]{2,1,0:T(8,128)(2,1)S(1)}, bf16[1,256,512]{2,1,0:T(8,128)(2,1)S(1)}, u32[]{:S(2)}, u32[]{:S(2)}) %collective-permute-start.1) | collective-permute-done | bytes 262176 | tf_op jit(solution)/shard_map/ppermute | solution.py:15
  17.4 1.2 select_maximum_fusion.9
  19.8 2.7 %fusion.10 = f32[2,256,512]{2,1,0:T(8,128)S(1)} fusion(bf16[2,256,4608]{2,1,0:T(8,128)(2,1)S(1)} %slice_dynamic-update-slice_fusion.18, bf16[4608,512,1]{1,0,2:T(8,128)(2,1)S(1)} %bitcast.78, f32[512]{0:T(512)S(1)} %bitcast.68), kind=kOutput, calls=%fused_computation.82 | convolution fusion | flops 2416967680 | bytes 10487808 | tf_op jit(solution)/shard_map/dot_general | solution.py:36
  22.7 4.9 %collective-permute-start.2 = (bf16[1,256,256]{2,1,0:T(8,128)(2,1)S(1)}, bf16[1,256,256]{2,1,0:T(8,128)(2,1)S(1)}, u32[]{:S(2)}, u32[]{:S(2)}) collective-permute-start(bf16[1,256,256]{2,1,0:T(8,128)(2,1)S(1)} %get-tuple-element.19), channel_id=1, source_target_pairs={{0,1},{1,2},{2,3},{3,4},{4,5},{5,6},{6,7},{7,8},{8,9},{9,10},{10,1... | collective-permute-start | bytes 393224 | tf_op jit(solution)/shard_map/ppermute | solution.py:12
  27.6 1.9 %collective-permute-start.3 = (bf16[1,256,256]{2,1,0:T(8,128)(2,1)S(1)}, bf16[1,256,256]{2,1,0:T(8,128)(2,1)S(1)}, u32[]{:S(2)}, u32[]{:S(2)}) collective-permute-start(bf16[1,256,256]{2,1,0:T(8,128)(2,1)S(1)} %get-tuple-element.20), channel_id=1, source_target_pairs={{1,0},{2,1},{3,2},{4,3},{5,4},{6,5},{7,6},{8,7},{9,8},{10,9},{11,1... | collective-permute-start | bytes 393224 | tf_op jit(solution)/shard_map/ppermute | solution.py:15
  30.3 6.0 %collective-permute-done.3 = bf16[1,256,256]{2,1,0:T(8,128)(2,1)S(1)} collective-permute-done((bf16[1,256,256]{2,1,0:T(8,128)(2,1)S(1)}, bf16[1,256,256]{2,1,0:T(8,128)(2,1)S(1)}, u32[]{:S(2)}, u32[]{:S(2)}) %collective-permute-start.3) | collective-permute-done | bytes 131104 | tf_op jit(solution)/shard_map/ppermute | solution.py:15
  37.4 1.4 broadcast_select_fusion.2
  38.8 1.3 collective-permute-start.4
  40.1 1.1 collective-permute-done.4
  41.3 2.3 %collective-permute-start.5 = (bf16[1,256,512]{2,1,0:T(8,128)(2,1)S(1)}, bf16[1,256,512]{2,1,0:T(8,128)(2,1)S(1)}, u32[]{:S(2)}, u32[]{:S(2)}) collective-permute-start(bf16[1,256,512]{2,1,0:T(8,128)(2,1)S(1)} %get-tuple-element.9), channel_id=1, source_target_pairs={{0,1},{1,2},{2,3},{3,4},{4,5},{5,6},{6,7},{7,8},{8,9},{9,10},{10,1... | collective-permute-start | bytes 786440 | tf_op jit(solution)/shard_map/ppermute | solution.py:12
  43.7 3.5 %collective-permute-start.6 = (bf16[1,256,512]{2,1,0:T(8,128)(2,1)S(1)}, bf16[1,256,512]{2,1,0:T(8,128)(2,1)S(1)}, u32[]{:S(2)}, u32[]{:S(2)}) collective-permute-start(bf16[1,256,512]{2,1,0:T(8,128)(2,1)S(1)} %get-tuple-element.10), channel_id=1, source_target_pairs={{1,0},{2,1},{3,2},{4,3},{5,4},{6,5},{7,6},{8,7},{9,8},{10,9},{11,1... | collective-permute-start | bytes 786440 | tf_op jit(solution)/shard_map/ppermute | solution.py:15
  47.2 5.2 %collective-permute-done.5 = bf16[1,256,512]{2,1,0:T(8,128)(2,1)S(1)} collective-permute-done((bf16[1,256,512]{2,1,0:T(8,128)(2,1)S(1)}, bf16[1,256,512]{2,1,0:T(8,128)(2,1)S(1)}, u32[]{:S(2)}, u32[]{:S(2)}) %collective-permute-start.5) | collective-permute-done | bytes 262176 | tf_op jit(solution)/shard_map/ppermute | solution.py:12
  52.4 3.3 %collective-permute-done.6 = bf16[1,256,512]{2,1,0:T(8,128)(2,1)S(1)} collective-permute-done((bf16[1,256,512]{2,1,0:T(8,128)(2,1)S(1)}, bf16[1,256,512]{2,1,0:T(8,128)(2,1)S(1)}, u32[]{:S(2)}, u32[]{:S(2)}) %collective-permute-start.6) | collective-permute-done | bytes 262176 | tf_op jit(solution)/shard_map/ppermute | solution.py:15
  56.7 2.7 %fusion.12 = f32[2,256,512]{2,1,0:T(8,128)S(1)} fusion(bf16[2,256,4608]{2,1,0:T(8,128)(2,1)S(1)} %slice_dynamic-update-slice_fusion.12, bf16[4608,512,1]{1,0,2:T(8,128)(2,1)S(1)} %bitcast.79, f32[512]{0:T(512)S(1)} %bitcast.69), kind=kOutput, calls=%fused_computation.84 | convolution fusion | flops 2416967680 | bytes 10487808 | tf_op jit(solution)/shard_map/dot_general | solution.py:36
  61.1 5.1 %collective-permute-start.7 = (bf16[1,256,256]{2,1,0:T(8,128)(2,1)}, bf16[1,256,256]{2,1,0:T(8,128)(2,1)}, u32[]{:S(2)}, u32[]{:S(2)}) collective-permute-start(bf16[1,256,256]{2,1,0:T(8,128)(2,1)} %get-tuple-element.17), channel_id=1, source_target_pairs={{0,1},{1,2},{2,3},{3,4},{4,5},{5,6},{6,7},{7,8},{8,9},{9,10},{10,1... | collective-permute-start | bytes 393224 | tf_op jit(solution)/shard_map/ppermute | solution.py:12
  66.3 1.9 %collective-permute-start.8 = (bf16[1,256,256]{2,1,0:T(8,128)(2,1)}, bf16[1,256,256]{2,1,0:T(8,128)(2,1)}, u32[]{:S(2)}, u32[]{:S(2)}) collective-permute-start(bf16[1,256,256]{2,1,0:T(8,128)(2,1)} %get-tuple-element.18), channel_id=1, source_target_pairs={{1,0},{2,1},{3,2},{4,3},{5,4},{6,5},{7,6},{8,7},{9,8},{10,9},{11,1... | collective-permute-start | bytes 393224 | tf_op jit(solution)/shard_map/ppermute | solution.py:15
  69.1 6.2 %collective-permute-done.8 = bf16[1,256,256]{2,1,0:T(8,128)(2,1)} collective-permute-done((bf16[1,256,256]{2,1,0:T(8,128)(2,1)}, bf16[1,256,256]{2,1,0:T(8,128)(2,1)}, u32[]{:S(2)}, u32[]{:S(2)}) %collective-permute-start.8) | collective-permute-done | bytes 131104 | tf_op jit(solution)/shard_map/ppermute | solution.py:15
  75.2 1.2 select_maximum_fusion.15
  78.0 1.4 broadcast_select_fusion.1
  79.5 1.3 collective-permute-start.9
  80.8 1.1 collective-permute-done.9
  81.9 1.1 bitcast_select_fusion.2
  83.1 2.3 %collective-permute-start.10 = (bf16[1,256,512]{2,1,0:T(8,128)(2,1)S(1)}, bf16[1,256,512]{2,1,0:T(8,128)(2,1)S(1)}, u32[]{:S(2)}, u32[]{:S(2)}) collective-permute-start(bf16[1,256,512]{2,1,0:T(8,128)(2,1)S(1)} %get-tuple-element.7), channel_id=1, source_target_pairs={{0,1},{1,2},{2,3},{3,4},{4,5},{5,6},{6,7},{7,8},{8,9},{9,10},{10,1... | collective-permute-start | bytes 786440 | tf_op jit(solution)/shard_map/ppermute | solution.py:12
  85.4 3.9 %collective-permute-start.11 = (bf16[1,256,512]{2,1,0:T(8,128)(2,1)S(1)}, bf16[1,256,512]{2,1,0:T(8,128)(2,1)S(1)}, u32[]{:S(2)}, u32[]{:S(2)}) collective-permute-start(bf16[1,256,512]{2,1,0:T(8,128)(2,1)S(1)} %get-tuple-element.8), channel_id=1, source_target_pairs={{1,0},{2,1},{3,2},{4,3},{5,4},{6,5},{7,6},{8,7},{9,8},{10,9},{11,1... | collective-permute-start | bytes 786440 | tf_op jit(solution)/shard_map/ppermute | solution.py:15
  89.3 5.0 %collective-permute-done.10 = bf16[1,256,512]{2,1,0:T(8,128)(2,1)S(1)} collective-permute-done((bf16[1,256,512]{2,1,0:T(8,128)(2,1)S(1)}, bf16[1,256,512]{2,1,0:T(8,128)(2,1)S(1)}, u32[]{:S(2)}, u32[]{:S(2)}) %collective-permute-start.10) | collective-permute-done | bytes 262176 | tf_op jit(solution)/shard_map/ppermute | solution.py:12
  94.3 3.2 %collective-permute-done.11 = bf16[1,256,512]{2,1,0:T(8,128)(2,1)S(1)} collective-permute-done((bf16[1,256,512]{2,1,0:T(8,128)(2,1)S(1)}, bf16[1,256,512]{2,1,0:T(8,128)(2,1)S(1)}, u32[]{:S(2)}, u32[]{:S(2)}) %collective-permute-start.11) | collective-permute-done | bytes 262176 | tf_op jit(solution)/shard_map/ppermute | solution.py:15
  99.0 2.7 %fusion.14 = f32[2,256,512]{2,1,0:T(8,128)S(1)} fusion(bf16[2,256,4608]{2,1,0:T(8,128)(2,1)S(1)} %slice_dynamic-update-slice_fusion.6, bf16[4608,512,1]{1,0,2:T(8,128)(2,1)S(1)} %bitcast.82, f32[512]{0:T(512)S(1)} %bitcast.70), kind=kOutput, calls=%fused_computation.86 | convolution fusion | flops 2416967680 | bytes 10487808 | tf_op jit(solution)/shard_map/dot_general | solution.py:36
  103.4 5.2 %collective-permute-start.12 = (bf16[1,256,256]{2,1,0:T(8,128)(2,1)}, bf16[1,256,256]{2,1,0:T(8,128)(2,1)}, u32[]{:S(2)}, u32[]{:S(2)}) collective-permute-start(bf16[1,256,256]{2,1,0:T(8,128)(2,1)} %get-tuple-element.15), channel_id=1, source_target_pairs={{0,1},{1,2},{2,3},{3,4},{4,5},{5,6},{6,7},{7,8},{8,9},{9,10},{10,1... | collective-permute-start | bytes 393224 | tf_op jit(solution)/shard_map/ppermute | solution.py:12
  108.6 1.9 %collective-permute-start.13 = (bf16[1,256,256]{2,1,0:T(8,128)(2,1)}, bf16[1,256,256]{2,1,0:T(8,128)(2,1)}, u32[]{:S(2)}, u32[]{:S(2)}) collective-permute-start(bf16[1,256,256]{2,1,0:T(8,128)(2,1)} %get-tuple-element.16), channel_id=1, source_target_pairs={{1,0},{2,1},{3,2},{4,3},{5,4},{6,5},{7,6},{8,7},{9,8},{10,9},{11,1... | collective-permute-start | bytes 393224 | tf_op jit(solution)/shard_map/ppermute | solution.py:15
  110.6 1.0 collective-permute-done.12
  111.6 6.0 %collective-permute-done.13 = bf16[1,256,256]{2,1,0:T(8,128)(2,1)} collective-permute-done((bf16[1,256,256]{2,1,0:T(8,128)(2,1)}, bf16[1,256,256]{2,1,0:T(8,128)(2,1)}, u32[]{:S(2)}, u32[]{:S(2)}) %collective-permute-start.13) | collective-permute-done | bytes 131104 | tf_op jit(solution)/shard_map/ppermute | solution.py:15
  117.6 1.2 select_maximum_fusion.13
  120.4 1.4 broadcast_select_fusion
  121.8 1.3 collective-permute-start.14
  125.3 2.4 %collective-permute-start.15 = (bf16[1,256,512]{2,1,0:T(8,128)(2,1)S(1)}, bf16[1,256,512]{2,1,0:T(8,128)(2,1)S(1)}, u32[]{:S(2)}, u32[]{:S(2)}) collective-permute-start(bf16[1,256,512]{2,1,0:T(8,128)(2,1)S(1)} %get-tuple-element.5), channel_id=1, source_target_pairs={{0,1},{1,2},{2,3},{3,4},{4,5},{5,6},{6,7},{7,8},{8,9},{9,10},{10,1... | collective-permute-start | bytes 786440 | tf_op jit(solution)/shard_map/ppermute | solution.py:12
  127.7 3.7 %collective-permute-start.16 = (bf16[1,256,512]{2,1,0:T(8,128)(2,1)S(1)}, bf16[1,256,512]{2,1,0:T(8,128)(2,1)S(1)}, u32[]{:S(2)}, u32[]{:S(2)}) collective-permute-start(bf16[1,256,512]{2,1,0:T(8,128)(2,1)S(1)} %get-tuple-element.6), channel_id=1, source_target_pairs={{1,0},{2,1},{3,2},{4,3},{5,4},{6,5},{7,6},{8,7},{9,8},{10,9},{11,1... | collective-permute-start | bytes 786440 | tf_op jit(solution)/shard_map/ppermute | solution.py:15
  131.6 5.1 %collective-permute-done.15 = bf16[1,256,512]{2,1,0:T(8,128)(2,1)S(1)} collective-permute-done((bf16[1,256,512]{2,1,0:T(8,128)(2,1)S(1)}, bf16[1,256,512]{2,1,0:T(8,128)(2,1)S(1)}, u32[]{:S(2)}, u32[]{:S(2)}) %collective-permute-start.15) | collective-permute-done | bytes 262176 | tf_op jit(solution)/shard_map/ppermute | solution.py:12
  136.6 3.2 %collective-permute-done.16 = bf16[1,256,512]{2,1,0:T(8,128)(2,1)S(1)} collective-permute-done((bf16[1,256,512]{2,1,0:T(8,128)(2,1)S(1)}, bf16[1,256,512]{2,1,0:T(8,128)(2,1)S(1)}, u32[]{:S(2)}, u32[]{:S(2)}) %collective-permute-start.16) | collective-permute-done | bytes 262176 | tf_op jit(solution)/shard_map/ppermute | solution.py:15
  141.3 2.7 %fusion.16 = f32[2,256,512]{2,1,0:T(8,128)S(1)} fusion(bf16[2,256,4608]{2,1,0:T(8,128)(2,1)S(1)} %slice_dynamic-update-slice_fusion, bf16[4608,512,1]{1,0,2:T(8,128)(2,1)S(1)} %bitcast.85, f32[512]{0:T(512)S(1)} %bitcast.71), kind=kOutput, calls=%fused_computation.88 | convolution fusion | flops 2416967680 | bytes 10487808 | tf_op jit(solution)/shard_map/dot_general | solution.py:36
  144.2 5.2 %collective-permute-start.17 = (bf16[1,256,256]{2,1,0:T(8,128)(2,1)S(1)}, bf16[1,256,256]{2,1,0:T(8,128)(2,1)S(1)}, u32[]{:S(2)}, u32[]{:S(2)}) collective-permute-start(bf16[1,256,256]{2,1,0:T(8,128)(2,1)S(1)} %get-tuple-element.13), channel_id=1, source_target_pairs={{0,1},{1,2},{2,3},{3,4},{4,5},{5,6},{6,7},{7,8},{8,9},{9,10},{10,1... | collective-permute-start | bytes 393224 | tf_op jit(solution)/shard_map/ppermute | solution.py:12
  149.3 1.9 %collective-permute-start.18 = (bf16[1,256,256]{2,1,0:T(8,128)(2,1)S(1)}, bf16[1,256,256]{2,1,0:T(8,128)(2,1)S(1)}, u32[]{:S(2)}, u32[]{:S(2)}) collective-permute-start(bf16[1,256,256]{2,1,0:T(8,128)(2,1)S(1)} %get-tuple-element.14), channel_id=1, source_target_pairs={{1,0},{2,1},{3,2},{4,3},{5,4},{6,5},{7,6},{8,7},{9,8},{10,9},{11,1... | collective-permute-start | bytes 393224 | tf_op jit(solution)/shard_map/ppermute | solution.py:15
  152.3 5.7 %collective-permute-done.18 = bf16[1,256,256]{2,1,0:T(8,128)(2,1)S(1)} collective-permute-done((bf16[1,256,256]{2,1,0:T(8,128)(2,1)S(1)}, bf16[1,256,256]{2,1,0:T(8,128)(2,1)S(1)}, u32[]{:S(2)}, u32[]{:S(2)}) %collective-permute-start.18) | collective-permute-done | bytes 131104 | tf_op jit(solution)/shard_map/ppermute | solution.py:15
  159.1 2.1 %fusion.35 = bf16[1,3,2,256,256]{4,3,2,1,0:T(8,128)(2,1)} fusion(bf16[1,3,2,256,256]{4,3,2,1,0:T(8,128)(2,1)} %copy.77, s32[]{:T(128)S(6)} %min.16, bf16[2,256,4608]{2,1,0:T(8,128)(2,1)S(1)} %fusion.108, bf16[4608,256,1]{1,0,2:T(8,128)(2,1)S(1)} %bitcast.62, bf16[2,256,256]{2,1,0:T(8,128)(2,1)S(1)} %get-tuple-element.25, f32[2,256,512]{2,1,0:T(8,128)S(1)} %fusion.16, ...), kind=kOutput, calls=%fused_computation.111 | convolution fusion | flops 1209008128 | bytes 8389637 | tf_op jit(solution)/shard_map/dot_general | solution.py:36
  (160 shorter events, 18.9 us)
Async XLA Ops:
  0.0 37.4 %copy-start = (bf16[1,3,3,512,256]{4,3,2,1,0:T(8,128)(2,1)S(1)}, bf16[1,3,3,512,256]{4,3,2,1,0:T(8,128)(2,1)}, u32[]{:S(2)}) copy-start(bf16[1,3,3,512,256]{4,3,2,1,0:T(8,128)(2,1)} %param.8) | copy-start | bytes 7077892
  0.0 19.0 %copy-start.8 = (bf16[3,2,256,256]{3,2,1,0:T(8,128)(2,1)S(1)}, bf16[3,2,256,256]{3,2,1,0:T(8,128)(2,1)}, u32[]{:S(2)}) copy-start(bf16[3,2,256,256]{3,2,1,0:T(8,128)(2,1)} %param.5) | copy-start | bytes 2359300
  0.0 18.7 %copy-start.1 = (bf16[1,2,256,256]{3,2,1,0:T(8,128)(2,1)S(1)}, bf16[1,2,256,256]{3,2,1,0:T(8,128)(2,1)}, u32[]{:S(2)}) copy-start(bf16[1,2,256,256]{3,2,1,0:T(8,128)(2,1)} %param.6) | copy-start | bytes 786436
  1.2 18.2 %slice-start = ((s8[4718592]{0:T(1024)(128)(4,1)}), s8[4194304]{0:T(1024)(128)(4,1)S(1)}, s32[]{:S(2)}) async-start(s8[4718592]{0:T(1024)(128)(4,1)} %bitcast.76), calls=%async_computation | async-start | bytes 8388608
  2.3 11.2 %collective-permute-start = (bf16[1,256,512]{2,1,0:T(8,128)(2,1)S(1)}, bf16[1,256,512]{2,1,0:T(8,128)(2,1)S(1)}, u32[]{:S(2)}, u32[]{:S(2)}) collective-permute-start(bf16[1,256,512]{2,1,0:T(8,128)(2,1)S(1)} %get-tuple-element.11), channel_id=1, source_target_pairs={{0,1},{1,2},{2,3},{3,4},{4,5},{5,6},{6,7},{7,8},{8,9},{9,10},{10,1... | collective-permute-start | bytes 786440 | tf_op jit(solution)/shard_map/ppermute | solution.py:12
  5.9 11.6 %collective-permute-start.1 = (bf16[1,256,512]{2,1,0:T(8,128)(2,1)S(1)}, bf16[1,256,512]{2,1,0:T(8,128)(2,1)S(1)}, u32[]{:S(2)}, u32[]{:S(2)}) collective-permute-start(bf16[1,256,512]{2,1,0:T(8,128)(2,1)S(1)} %get-tuple-element.12), channel_id=1, source_target_pairs={{1,0},{2,1},{3,2},{4,3},{5,4},{6,5},{7,6},{8,7},{9,8},{10,9},{11,1... | collective-permute-start | bytes 786440 | tf_op jit(solution)/shard_map/ppermute | solution.py:15
  18.8 1.0 slice-start.1
  22.7 7.6 %collective-permute-start.2 = (bf16[1,256,256]{2,1,0:T(8,128)(2,1)S(1)}, bf16[1,256,256]{2,1,0:T(8,128)(2,1)S(1)}, u32[]{:S(2)}, u32[]{:S(2)}) collective-permute-start(bf16[1,256,256]{2,1,0:T(8,128)(2,1)S(1)} %get-tuple-element.19), channel_id=1, source_target_pairs={{0,1},{1,2},{2,3},{3,4},{4,5},{5,6},{6,7},{7,8},{8,9},{9,10},{10,1... | collective-permute-start | bytes 393224 | tf_op jit(solution)/shard_map/ppermute | solution.py:12
  27.6 8.7 %collective-permute-start.3 = (bf16[1,256,256]{2,1,0:T(8,128)(2,1)S(1)}, bf16[1,256,256]{2,1,0:T(8,128)(2,1)S(1)}, u32[]{:S(2)}, u32[]{:S(2)}) collective-permute-start(bf16[1,256,256]{2,1,0:T(8,128)(2,1)S(1)} %get-tuple-element.20), channel_id=1, source_target_pairs={{1,0},{2,1},{3,2},{4,3},{5,4},{6,5},{7,6},{8,7},{9,8},{10,9},{11,1... | collective-permute-start | bytes 393224 | tf_op jit(solution)/shard_map/ppermute | solution.py:15
  38.8 17.6 %copy-start.13 = (bf16[2,256,256]{2,1,0:T(8,128)(2,1)}, bf16[2,256,256]{2,1,0:T(8,128)(2,1)S(1)}, u32[]{:S(2)}) copy-start(bf16[2,256,256]{2,1,0:T(8,128)(2,1)S(1)} %get-tuple-element.22) | copy-start | bytes 786436
  38.8 20.6 %copy-start.4 = (bf16[2,256,256]{2,1,0:T(8,128)(2,1)}, bf16[2,256,256]{2,1,0:T(8,128)(2,1)S(1)}, u32[]{:S(2)}) copy-start(bf16[2,256,256]{2,1,0:T(8,128)(2,1)S(1)} %get-tuple-element.21) | copy-start | bytes 786436
  38.8 2.4 %collective-permute-start.4 = (bf16[2,256,256]{2,1,0:T(8,128)(2,1)S(1)}, bf16[2,256,256]{2,1,0:T(8,128)(2,1)S(1)}, u32[]{:S(2)}, u32[]{:S(2)}) collective-permute-start(bf16[2,256,256]{2,1,0:T(8,128)(2,1)S(1)} %get-tuple-element.22), channel_id=1, source_target_pairs={{0,16},{1,17},{2,18},{3,19},{4,20},{5,21},{6,22},{7,23},{8,24},{9,... | collective-permute-start | bytes 786440 | tf_op jit(solution)/shard_map/ppermute | solution.py:23
  41.3 11.1 %collective-permute-start.5 = (bf16[1,256,512]{2,1,0:T(8,128)(2,1)S(1)}, bf16[1,256,512]{2,1,0:T(8,128)(2,1)S(1)}, u32[]{:S(2)}, u32[]{:S(2)}) collective-permute-start(bf16[1,256,512]{2,1,0:T(8,128)(2,1)S(1)} %get-tuple-element.9), channel_id=1, source_target_pairs={{0,1},{1,2},{2,3},{3,4},{4,5},{5,6},{6,7},{7,8},{8,9},{9,10},{10,1... | collective-permute-start | bytes 786440 | tf_op jit(solution)/shard_map/ppermute | solution.py:12
  43.7 12.1 %collective-permute-start.6 = (bf16[1,256,512]{2,1,0:T(8,128)(2,1)S(1)}, bf16[1,256,512]{2,1,0:T(8,128)(2,1)S(1)}, u32[]{:S(2)}, u32[]{:S(2)}) collective-permute-start(bf16[1,256,512]{2,1,0:T(8,128)(2,1)S(1)} %get-tuple-element.10), channel_id=1, source_target_pairs={{1,0},{2,1},{3,2},{4,3},{5,4},{6,5},{7,6},{8,7},{9,8},{10,9},{11,1... | collective-permute-start | bytes 786440 | tf_op jit(solution)/shard_map/ppermute | solution.py:15
  59.5 1.7 %copy-start.11 = (f32[2,256,512]{2,1,0:T(8,128)}, f32[2,256,512]{2,1,0:T(8,128)S(1)}, u32[]{:S(2)}) copy-start(f32[2,256,512]{2,1,0:T(8,128)S(1)} %fusion.12) | copy-start | bytes 3145732
  59.6 0.8 copy-start.7
  61.1 7.9 %collective-permute-start.7 = (bf16[1,256,256]{2,1,0:T(8,128)(2,1)}, bf16[1,256,256]{2,1,0:T(8,128)(2,1)}, u32[]{:S(2)}, u32[]{:S(2)}) collective-permute-start(bf16[1,256,256]{2,1,0:T(8,128)(2,1)} %get-tuple-element.17), channel_id=1, source_target_pairs={{0,1},{1,2},{2,3},{3,4},{4,5},{5,6},{6,7},{7,8},{8,9},{9,10},{10,1... | collective-permute-start | bytes 393224 | tf_op jit(solution)/shard_map/ppermute | solution.py:12
  66.3 9.0 %collective-permute-start.8 = (bf16[1,256,256]{2,1,0:T(8,128)(2,1)}, bf16[1,256,256]{2,1,0:T(8,128)(2,1)}, u32[]{:S(2)}, u32[]{:S(2)}) collective-permute-start(bf16[1,256,256]{2,1,0:T(8,128)(2,1)} %get-tuple-element.18), channel_id=1, source_target_pairs={{1,0},{2,1},{3,2},{4,3},{5,4},{6,5},{7,6},{8,7},{9,8},{10,9},{11,1... | collective-permute-start | bytes 393224 | tf_op jit(solution)/shard_map/ppermute | solution.py:15
  76.7 1.0 copy-start.5
  76.7 1.3 copy-start.12
  79.5 18.7 %copy-start.15 = (bf16[2,256,256]{2,1,0:T(8,128)(2,1)}, bf16[2,256,256]{2,1,0:T(8,128)(2,1)S(1)}, u32[]{:S(2)}) copy-start(bf16[2,256,256]{2,1,0:T(8,128)(2,1)S(1)} %get-tuple-element.24) | copy-start | bytes 786436
  79.5 22.2 %copy-start.2 = (bf16[2,256,256]{2,1,0:T(8,128)(2,1)}, bf16[2,256,256]{2,1,0:T(8,128)(2,1)S(1)}, u32[]{:S(2)}) copy-start(bf16[2,256,256]{2,1,0:T(8,128)(2,1)S(1)} %get-tuple-element.23) | copy-start | bytes 786436
  79.5 2.4 %collective-permute-start.9 = (bf16[2,256,256]{2,1,0:T(8,128)(2,1)S(1)}, bf16[2,256,256]{2,1,0:T(8,128)(2,1)S(1)}, u32[]{:S(2)}, u32[]{:S(2)}) collective-permute-start(bf16[2,256,256]{2,1,0:T(8,128)(2,1)S(1)} %get-tuple-element.24), channel_id=1, source_target_pairs={{0,16},{1,17},{2,18},{3,19},{4,20},{5,21},{6,22},{7,23},{8,24},{9,... | collective-permute-start | bytes 786440 | tf_op jit(solution)/shard_map/ppermute | solution.py:23
  81.9 16.6 %slice-start.2 = ((s8[4718592]{0:T(1024)(128)(4,1)}), s8[4194304]{0:T(1024)(128)(4,1)S(1)}, s32[]{:S(2)}) async-start(s8[4718592]{0:T(1024)(128)(4,1)} %bitcast.80), calls=%async_computation.2 | async-start | bytes 8388608
  83.1 11.2 %collective-permute-start.10 = (bf16[1,256,512]{2,1,0:T(8,128)(2,1)S(1)}, bf16[1,256,512]{2,1,0:T(8,128)(2,1)S(1)}, u32[]{:S(2)}, u32[]{:S(2)}) collective-permute-start(bf16[1,256,512]{2,1,0:T(8,128)(2,1)S(1)} %get-tuple-element.7), channel_id=1, source_target_pairs={{0,1},{1,2},{2,3},{3,4},{4,5},{5,6},{6,7},{7,8},{8,9},{9,10},{10,1... | collective-permute-start | bytes 786440 | tf_op jit(solution)/shard_map/ppermute | solution.py:12
  85.4 12.1 %collective-permute-start.11 = (bf16[1,256,512]{2,1,0:T(8,128)(2,1)S(1)}, bf16[1,256,512]{2,1,0:T(8,128)(2,1)S(1)}, u32[]{:S(2)}, u32[]{:S(2)}) collective-permute-start(bf16[1,256,512]{2,1,0:T(8,128)(2,1)S(1)} %get-tuple-element.8), channel_id=1, source_target_pairs={{1,0},{2,1},{3,2},{4,3},{5,4},{6,5},{7,6},{8,7},{9,8},{10,9},{11,1... | collective-permute-start | bytes 786440 | tf_op jit(solution)/shard_map/ppermute | solution.py:15
  97.9 1.0 slice-start.3
  101.7 1.7 %copy-start.9 = (f32[2,256,512]{2,1,0:T(8,128)}, f32[2,256,512]{2,1,0:T(8,128)S(1)}, u32[]{:S(2)}) copy-start(f32[2,256,512]{2,1,0:T(8,128)S(1)} %fusion.14) | copy-start | bytes 3145732
  101.8 0.9 copy-start.6
  103.4 8.2 %collective-permute-start.12 = (bf16[1,256,256]{2,1,0:T(8,128)(2,1)}, bf16[1,256,256]{2,1,0:T(8,128)(2,1)}, u32[]{:S(2)}, u32[]{:S(2)}) collective-permute-start(bf16[1,256,256]{2,1,0:T(8,128)(2,1)} %get-tuple-element.15), channel_id=1, source_target_pairs={{0,1},{1,2},{2,3},{3,4},{4,5},{5,6},{6,7},{7,8},{8,9},{9,10},{10,1... | collective-permute-start | bytes 393224 | tf_op jit(solution)/shard_map/ppermute | solution.py:12
  108.6 9.0 %collective-permute-start.13 = (bf16[1,256,256]{2,1,0:T(8,128)(2,1)}, bf16[1,256,256]{2,1,0:T(8,128)(2,1)}, u32[]{:S(2)}, u32[]{:S(2)}) collective-permute-start(bf16[1,256,256]{2,1,0:T(8,128)(2,1)} %get-tuple-element.16), channel_id=1, source_target_pairs={{1,0},{2,1},{3,2},{4,3},{5,4},{6,5},{7,6},{8,7},{9,8},{10,9},{11,1... | collective-permute-start | bytes 393224 | tf_op jit(solution)/shard_map/ppermute | solution.py:15
  119.1 1.0 copy-start.3
  119.1 1.3 copy-start.10
  120.4 2.8 %copy-start.14 = (bf16[2,256,256]{2,1,0:T(8,128)(2,1)S(1)}, bf16[2,256,256]{2,1,0:T(8,128)(2,1)}, u32[]{:S(2)}) copy-start(bf16[2,256,256]{2,1,0:T(8,128)(2,1)} %copy-done.13) | copy-start | bytes 786436
  120.4 11.0 %copy-start.16 = (bf16[2,256,256]{2,1,0:T(8,128)(2,1)S(1)}, bf16[2,256,256]{2,1,0:T(8,128)(2,1)}, u32[]{:S(2)}) copy-start(bf16[2,256,256]{2,1,0:T(8,128)(2,1)} %copy-done.15) | copy-start | bytes 786436
  121.8 2.4 %collective-permute-start.14 = (bf16[2,256,256]{2,1,0:T(8,128)(2,1)S(1)}, bf16[2,256,256]{2,1,0:T(8,128)(2,1)S(1)}, u32[]{:S(2)}, u32[]{:S(2)}) collective-permute-start(bf16[2,256,256]{2,1,0:T(8,128)(2,1)S(1)} %get-tuple-element.26), channel_id=1, source_target_pairs={{0,16},{1,17},{2,18},{3,19},{4,20},{5,21},{6,22},{7,23},{8,24},{9,... | collective-permute-start | bytes 786440 | tf_op jit(solution)/shard_map/ppermute | solution.py:23
  125.3 15.6 %slice-start.4 = ((s8[4718592]{0:T(1024)(128)(4,1)}), s8[4194304]{0:T(1024)(128)(4,1)S(1)}, s32[]{:S(2)}) async-start(s8[4718592]{0:T(1024)(128)(4,1)} %bitcast.83), calls=%async_computation.4 | async-start | bytes 8388608
  125.3 11.3 %collective-permute-start.15 = (bf16[1,256,512]{2,1,0:T(8,128)(2,1)S(1)}, bf16[1,256,512]{2,1,0:T(8,128)(2,1)S(1)}, u32[]{:S(2)}, u32[]{:S(2)}) collective-permute-start(bf16[1,256,512]{2,1,0:T(8,128)(2,1)S(1)} %get-tuple-element.5), channel_id=1, source_target_pairs={{0,1},{1,2},{2,3},{3,4},{4,5},{5,6},{6,7},{7,8},{8,9},{9,10},{10,1... | collective-permute-start | bytes 786440 | tf_op jit(solution)/shard_map/ppermute | solution.py:12
  127.7 12.2 %collective-permute-start.16 = (bf16[1,256,512]{2,1,0:T(8,128)(2,1)S(1)}, bf16[1,256,512]{2,1,0:T(8,128)(2,1)S(1)}, u32[]{:S(2)}, u32[]{:S(2)}) collective-permute-start(bf16[1,256,512]{2,1,0:T(8,128)(2,1)S(1)} %get-tuple-element.6), channel_id=1, source_target_pairs={{1,0},{2,1},{3,2},{4,3},{5,4},{6,5},{7,6},{8,7},{9,8},{10,9},{11,1... | collective-permute-start | bytes 786440 | tf_op jit(solution)/shard_map/ppermute | solution.py:15
  140.2 1.0 slice-start.5
  144.2 8.1 %collective-permute-start.17 = (bf16[1,256,256]{2,1,0:T(8,128)(2,1)S(1)}, bf16[1,256,256]{2,1,0:T(8,128)(2,1)S(1)}, u32[]{:S(2)}, u32[]{:S(2)}) collective-permute-start(bf16[1,256,256]{2,1,0:T(8,128)(2,1)S(1)} %get-tuple-element.13), channel_id=1, source_target_pairs={{0,1},{1,2},{2,3},{3,4},{4,5},{5,6},{6,7},{7,8},{8,9},{9,10},{10,1... | collective-permute-start | bytes 393224 | tf_op jit(solution)/shard_map/ppermute | solution.py:12
  149.3 8.7 %collective-permute-start.18 = (bf16[1,256,256]{2,1,0:T(8,128)(2,1)S(1)}, bf16[1,256,256]{2,1,0:T(8,128)(2,1)S(1)}, u32[]{:S(2)}, u32[]{:S(2)}) collective-permute-start(bf16[1,256,256]{2,1,0:T(8,128)(2,1)S(1)} %get-tuple-element.14), channel_id=1, source_target_pairs={{1,0},{2,1},{3,2},{4,3},{5,4},{6,5},{7,6},{8,7},{9,8},{10,9},{11,1... | collective-permute-start | bytes 393224 | tf_op jit(solution)/shard_map/ppermute | solution.py:15
where the time goes:
time: 162 us; the launch traced here: 161 us
  waiting for transfers between devices  62.5 us (39%)
  starting transfers between devices  56.1 us (35%)
  matrix products  17.3 us (11%)
  other arithmetic  13.6 us (8%)
  local copies, waits for them, and re-layouts  10.5 us (6%)
    ppermute x8, waiting for transfers between devices, with_halo(): lax.ppermute(lax.slice_in_dim(block, 0, width, axis=dim), axis, backward)  37.5 us
    ppermute x8, starting transfers between devices, with_halo(): lax.ppermute(lax.slice_in_dim(block, block.shape[dim] - width, None, axis...  30.9 us
    ppermute x8, waiting for transfers between devices, with_halo(): lax.ppermute(lax.slice_in_dim(block, block.shape[dim] - width, None, axis...  21.7 us
    ppermute x8, starting transfers between devices, with_halo(): lax.ppermute(lax.slice_in_dim(block, 0, width, axis=dim), axis, backward)  21.3 us
    dot_general x8, matrix products, convolve(): jnp.dot(stacked, weight_flat, preferred_element_type=jnp.float32)  17.3 us
    unnamed x74, local copies, waits for them, and re-layouts  6.86 us
    concatenate x8, other arithmetic, with_halo(): block = jnp.concatenate([low, block, high], axis=dim)  4.66 us
    ppermute x3, starting transfers between devices, shifted(): return lax.ppermute(block, axis, route)  3.92 us
  transfers between devices with their start and end apart: 19, of which 17 were waited for; matrix products, arithmetic and copies ran while one was open for 2% of the time, Pallas kernels for 0%

commit v1 on v0

v1 whole, which is shorter than its diff:
```python
import functools

import jax
import jax.numpy as jnp
from jax import lax
from jax.experimental import pallas as pl
from jax.experimental.pallas import tpu as pltpu
from jax.sharding import PartitionSpec as P

MESH = pltpu.DeviceIdType.MESH if hasattr(pltpu, "DeviceIdType") else pl.DeviceIdType.MESH

COL_DIRS = ((0, -1), (0, 1), (-1, -1), (-1, 1), (1, -1), (1, 1))


def reorder(c, group):
    if group == 4:
        return c + (c // 2) * (5 - 2 * c)
    return c


def kernel(
    count, group, frames_ref, init_ref, wg_ref, wc_ref, bias_ref, out_ref,
    wg, wc, xs, hs, rs, im, upd, part,
    row_halo, rs_row_halo, col_stage, col_halo, rs_col_stage, rs_col_halo,
    w_sem, own_sem, init_send, init_recv, x_send, x_recv, pass_send, pass_recv,
    out_own, out_send, out_recv,
    row_send, row_recv, col_send, col_recv,
    rrow_send, rrow_recv, rcol_send, rcol_recv,
):
    frame_count, strip, cols, ch = frames_ref.shape
    height = strip * group
    width = cols // group
    tile = height * width
    layer = lax.axis_index("layer")
    last_layer = lax.axis_size("layer") - 1
    index = lax.axis_index("rows")
    planes = count // group
    q = index // group
    c = index % group
    t = reorder(c, group)

    def at(plane, tile_index):
        return {"rows": plane * group + reorder(tile_index, group)}

    def guarded(step_row, step_col, action):
        terms = []
        if step_row < 0:
            terms.append(q > 0)
        if step_row > 0:
            terms.append(q < planes - 1)
        if step_col < 0:
            terms.append(t > 0)
        if step_col > 0:
            terms.append(t < group - 1)
        cond = functools.reduce(jnp.logical_and, terms)
        pl.when(cond)(action)

    copy_wg = pltpu.make_async_copy(wg_ref, wg, w_sem.at[0])
    copy_wc = pltpu.make_async_copy(wc_ref, wc, w_sem.at[1])
    own_cols = pl.ds(pl.multiple_of(t * width, width), width)
    own_rows = pl.ds(c * strip, strip)

    def own_init():
        return pltpu.make_async_copy(init_ref.at[:, own_cols, :], hs.at[0, own_rows], own_sem.at[0])

    def own_frame(f):
        return pltpu.make_async_copy(
            frames_ref.at[f, :, own_cols, :], xs.at[f, own_rows], own_sem.at[1]
        )

    def member(d):
        return lax.rem(c + d, group)

    def init_copy(d):
        target = member(d)
        tcols = pl.ds(pl.multiple_of(reorder(target, group) * width, width), width)
        return pltpu.make_async_remote_copy(
            src_ref=init_ref.at[:, tcols, :], dst_ref=hs.at[0, own_rows],
            send_sem=init_send.at[d], recv_sem=init_recv.at[d],
            device_id={"rows": q * group + target}, device_id_type=MESH,
        )

    def frame_copy(f, d):
        target = member(d)
        tcols = pl.ds(pl.multiple_of(reorder(target, group) * width, width), width)
        return pltpu.make_async_remote_copy(
            src_ref=frames_ref.at[f, :, tcols, :], dst_ref=xs.at[f, own_rows],
            send_sem=x_send.at[f, d], recv_sem=x_recv.at[f, d],
            device_id={"rows": q * group + target}, device_id_type=MESH,
        )

    def pass_copy(f):
        return pltpu.make_async_remote_copy(
            src_ref=hs.at[f + 1], dst_ref=xs.at[f],
            send_sem=pass_send.at[f], recv_sem=pass_recv.at[f],
            device_id={"layer": jnp.minimum(layer + 1, last_layer)}, device_id_type=MESH,
        )

    def out_copy(f, d):
        target = member(d)
        return pltpu.make_async_remote_copy(
            src_ref=hs.at[f + 1, pl.ds(target * strip, strip)],
            dst_ref=out_ref.at[0, f, :, own_cols, :],
            send_sem=out_send.at[f, d], recv_sem=out_recv.at[f, d],
            device_id={"rows": q * group + target}, device_id_type=MESH,
        )

    def own_out(f):
        return pltpu.make_async_copy(
            hs.at[f + 1, own_rows], out_ref.at[0, f, :, own_cols, :], out_own.at[f]
        )

    copy_wg.start()
    copy_wc.start()
    own_init().start()
    pl.when(layer == 0)(lambda: own_frame(0).start())

    row_halo[...] = jnp.zeros_like(row_halo)
    rs_row_halo[...] = jnp.zeros_like(rs_row_halo)
    col_halo[...] = jnp.zeros_like(col_halo)
    rs_col_halo[...] = jnp.zeros_like(rs_col_halo)

    barrier = pltpu.get_barrier_semaphore()

    def greet(where):
        pl.semaphore_signal(barrier, inc=1, device_id=where, device_id_type=MESH)

    for d in range(1, group):
        greet({"rows": q * group + member(d)})
    for step in (-1, 1):
        for side in (-1, 0, 1):
            guarded(step, side, lambda step=step, side=side: greet(at(q + step, t + side)))
    pl.when(layer > 0)(lambda: greet({"layer": layer - 1}))
    pl.when(layer < last_layer)(lambda: greet({"layer": layer + 1}))
    one = lambda cond: jnp.where(cond, 1, 0)
    sideways = 1 + one(t > 0) + one(t < group - 1)
    upright = one(q > 0) + one(q < planes - 1)
    pl.semaphore_wait(
        barrier, group - 1 + sideways * upright + one(layer > 0) + one(layer < last_layer)
    )

    for d in range(1, group):
        init_copy(d).start()

    @pl.when(layer == 0)
    def _():
        for d in range(1, group):
            frame_copy(0, d).start()

    own_init().wait()
    for d in range(1, group):
        init_copy(d).wait()

    def exchange(row_pairs, row_out, row_in, stage, halo, col_out, col_in, start):
        def run(copy):
            if start:
                copy.start()
            else:
                copy.wait()

        for side, step in enumerate((-1, 1)):
            for kind, (field, dest) in enumerate(row_pairs):
                def row(side=side, step=step, kind=kind, field=field, dest=dest):
                    run(pltpu.make_async_remote_copy(
                        src_ref=field.at[0 if step < 0 else height - 1],
                        dst_ref=dest.at[1 - side],
                        send_sem=row_out.at[kind, side], recv_sem=row_in.at[kind, 1 - side],
                        device_id=at(q + step, t), device_id_type=MESH,
                    ))

                if start:
                    guarded(step, 0, row)
                else:
                    def both(side=side, step=step, kind=kind, field=field, dest=dest):
                        copy = pltpu.make_async_remote_copy(
                            src_ref=field.at[0], dst_ref=dest.at[side],
                            send_sem=row_out.at[kind, side], recv_sem=row_in.at[kind, side],
                            device_id=at(q + step, t), device_id_type=MESH,
                        )
                        copy.wait()

                    guarded(step, 0, both)
        for k, (dr, dc) in enumerate(COL_DIRS):
            back = COL_DIRS.index((-dr, -dc))

            def col(k=k, back=back, dr=dr, dc=dc):
                copy = pltpu.make_async_remote_copy(
                    src_ref=stage.at[0 if dc < 0 else 1],
                    dst_ref=halo.at[back if start else k],
                    send_sem=col_out.at[k], recv_sem=col_in.at[back if start else k],
                    device_id=at(q + dr, t + dc), device_id_type=MESH,
                )
                run(copy)

            guarded(dr, dc, col)

    first_col = lax.broadcasted_iota(jnp.int32, (width, ch), 0) == 0
    last_col = lax.broadcasted_iota(jnp.int32, (width, ch), 0) == width - 1

    def spread(load, halo, lanes, base):
        for i in range(height + 2):
            v = load(i).astype(jnp.float32)
            if i == 0:
                left = halo[2, height - 1 : height, lanes]
                right = halo[3, height - 1 : height, lanes]
            elif i == height + 1:
                left, right = halo[4, 0:1, lanes], halo[5, 0:1, lanes]
            else:
                left, right = halo[0, i - 1 : i, lanes], halo[1, i - 1 : i, lanes]
            before = jnp.where(first_col, jnp.broadcast_to(left, v.shape), pltpu.roll(v, 1, 0))
            after = jnp.where(
                last_col, jnp.broadcast_to(right, v.shape), pltpu.roll(v, width - 1, 0)
            )
            rows = slice(i * width, (i + 1) * width)
            for b, piece in enumerate((before, v, after)):
                lo = b * 2 * ch + base
                im[rows, lo : lo + ch] = piece.astype(jnp.bfloat16)

    def lhs(a, lo, size):
        return im[a * width : a * width + tile, lo : lo + size]

    def full(weight, n_lo):
        total = None
        for a in range(3):
            term = jnp.dot(
                lhs(a, 0, 6 * ch), weight[a, :, n_lo : n_lo + ch],
                preferred_element_type=jnp.float32,
            )
            total = term if total is None else total + term
        return total

    def half(weight, base):
        total = None
        for a in range(3):
            for b in range(3):
                lo = b * 2 * ch + base
                term = jnp.dot(
                    lhs(a, lo, ch), weight[a, lo : lo + ch, :],
                    preferred_element_type=jnp.float32,
                )
                total = term if total is None else total + term
        return total

    def step(f, carry):
        @pl.when(layer == 0)
        def _():
            own_frame(f).wait()
            for d in range(1, group):
                frame_copy(f, d).wait()

        @pl.when(layer > 0)
        def _():
            pass_copy(f).wait_recv()

        for i in range(height):
            for k, field in enumerate((xs.at[f], hs.at[f])):
                v = field[i].astype(jnp.float32)
                lanes = slice(k * ch, (k + 1) * ch)
                col_stage[0, i : i + 1, lanes] = v[0:1]
                col_stage[1, i : i + 1, lanes] = v[width - 1 : width]
        args = (
            ((xs.at[f], row_halo.at[0]), (hs.at[f], row_halo.at[1])),
            row_send, row_recv, col_stage, col_halo, col_send, col_recv,
        )
        exchange(*args, True)
        exchange(*args, False)

        @pl.when(jnp.logical_and(layer == 0, f + 1 < frame_count))
        def _():
            own_frame(f + 1).start()
            for d in range(1, group):
                frame_copy(f + 1, d).start()

        for k, field in enumerate((xs, hs)):
            def load(i, k=k, field=field):
                if i == 0:
                    return row_halo[k, 0]
                if i == height + 1:
                    return row_halo[k, 1]
                return field[f, i - 1]

            spread(load, col_halo, slice(k * ch, (k + 1) * ch), k * ch)

        pl.when(f == 0)(lambda: copy_wg.wait())
        reset = jax.nn.sigmoid(full(wg, ch) + bias_ref[:, ch : 2 * ch])
        hidden = hs[f].reshape(tile, ch).astype(jnp.float32)
        rs[...] = (reset * hidden).astype(jnp.bfloat16).reshape(height, width, ch)
        for i in range(height):
            v = rs[i].astype(jnp.float32)
            rs_col_stage[0, i : i + 1, :] = v[0:1]
            rs_col_stage[1, i : i + 1, :] = v[width - 1 : width]
        args = (
            ((rs, rs_row_halo),),
            rrow_send, rrow_recv, rs_col_stage, rs_col_halo, rcol_send, rcol_recv,
        )
        exchange(*args, True)
        upd[...] = jax.nn.sigmoid(full(wg, 0) + bias_ref[:, 0:ch])
        pl.when(f == 0)(lambda: copy_wc.wait())
        part[...] = half(wc, 0) + bias_ref[:, 2 * ch : 3 * ch]
        exchange(*args, False)

        def load_reset(i):
            if i == 0:
                return rs_row_halo[0]
            if i == height + 1:
                return rs_row_halo[1]
            return rs[i - 1]

        spread(load_reset, rs_col_halo, slice(0, ch), ch)
        candidate = jnp.tanh(part[...] + half(wc, ch))
        update = upd[...]
        hidden = hs[f].reshape(tile, ch).astype(jnp.float32)
        fresh = (1.0 - update) * hidden + update * candidate
        hs[f + 1] = fresh.astype(jnp.bfloat16).reshape(height, width, ch)
        pl.when(layer < last_layer)(lambda: pass_copy(f).start())
        own_out(f).start()
        for d in range(1, group):
            out_copy(f, d).start()
        return carry

    lax.fori_loop(0, frame_count, step, 0)

    def finish(f, carry):
        pl.when(layer < last_layer)(lambda: pass_copy(f).wait_send())
        own_out(f).wait()
        for d in range(1, group):
            out_copy(f, d).wait()
        return carry

    lax.fori_loop(0, frame_count, finish, 0)


def shards(count, frames, initial_state, w_gates, w_cand, biases):
    frame_count, strip, cols, ch = frames.shape
    group = 4 if count % 4 == 0 else 1
    height, width = strip * group, cols // group
    dma = pltpu.SemaphoreType.DMA
    bf16, f32 = jnp.bfloat16, jnp.float32
    anywhere = pl.BlockSpec(memory_space=pl.ANY)
    rows_k = w_gates.shape[2] * w_gates.shape[3]
    tile = height * width
    return pl.pallas_call(
        functools.partial(kernel, count, group),
        out_shape=jax.ShapeDtypeStruct((1, frame_count, strip, cols, ch), bf16),
        in_specs=[anywhere] * 4 + [pl.BlockSpec(memory_space=pltpu.VMEM)],
        out_specs=anywhere,
        scratch_shapes=[
            pltpu.VMEM((3, rows_k, 2 * ch), bf16),
            pltpu.VMEM((3, rows_k, ch), bf16),
            pltpu.VMEM((frame_count, height, width, ch), bf16),
            pltpu.VMEM((frame_count + 1, height, width, ch), bf16),
            pltpu.VMEM((height, width, ch), bf16),
            pltpu.VMEM(((height + 2) * width, 6 * ch), bf16),
            pltpu.VMEM((tile, ch), f32),
            pltpu.VMEM((tile, ch), f32),
            pltpu.VMEM((2, 2, width, ch), bf16),
            pltpu.VMEM((2, width, ch), bf16),
            pltpu.VMEM((2, height, 2 * ch), f32),
            pltpu.VMEM((6, height, 2 * ch), f32),
            pltpu.VMEM((2, height, ch), f32),
            pltpu.VMEM((6, height, ch), f32),
            dma((2,)), dma((2,)), dma((group,)), dma((group,)),
            dma((frame_count, group)), dma((frame_count, group)),
            dma((frame_count,)), dma((frame_count,)),
            dma((frame_count,)), dma((frame_count, group)), dma((frame_count, group)),
            dma((2, 2)), dma((2, 2)), dma((6,)), dma((6,)),
            dma((1, 2)), dma((1, 2)), dma((6,)), dma((6,)),
        ],
        compiler_params=pltpu.CompilerParams(
            collective_id=0, has_side_effects=True, vmem_limit_bytes=48 * 1024 * 1024
        ),
    )(
        frames,
        initial_state[0],
        w_gates.reshape(3, rows_k, 2 * ch),
        w_cand.reshape(3, rows_k, ch),
        biases,
    )


def solution(mesh):
    placed = (
        P(None, "rows", None, None),
        P("layer", "rows", None, None),
        P("layer", None, None, None, None),
        P("layer", None, None, None, None),
        P("layer", None),
    )
    return jax.shard_map(
        functools.partial(shards, mesh.shape["rows"]),
        mesh=mesh,
        in_specs=placed,
        out_specs=P("layer", None, "rows", None, None),
        check_vma=False,
    )
```

time: 162 us -> 68.7 us (0.42)
  the two profiles are of different devices: /device:TPU:22 before, /device:TPU:1 now
where the time goes in v1:
time: 68.7 us; the launch traced here: 68.5 us
  Pallas kernels  63.2 us (92%)
  local copies, waits for them, and re-layouts  5.31 us (8%)
    pallas_call x1, Pallas kernels, shards(): pl.pallas_call(functools.partial(kernel, count, group), out_shape=jax.Sha...  63.2 us
    unnamed x9, local copies, waits for them, and re-layouts  5.31 us

profile of v1, /device:TPU:1, one launch (start us, length us, event | category | flops | bytes accessed | tf_op | source)
XLA Modules:
  0.0 68.5 jit_solution(1792309652962035789)
XLA Ops:
  0.0 0.0 copy-start
  0.0 1.7 %copy-done = bf16[1,3,3,512,256]{4,3,2,1,0:T(8,128)(2,1)S(1)} copy-done((bf16[1,3,3,512,256]{4,3,2,1,0:T(8,128)(2,1)S(1)}, bf16[1,3,3,512,256]{4,3,2,1,0:T(8,128)(2,1)}, u32[]{:S(2)}) %copy-start) | copy-done | bytes 2359320
  1.7 0.0 copy-start.1
  1.7 1.1 %copy-done.1 = bf16[3,2,256,256]{3,2,1,0:T(8,128)(2,1)S(1)} copy-done((bf16[3,2,256,256]{3,2,1,0:T(8,128)(2,1)S(1)}, bf16[3,2,256,256]{3,2,1,0:T(8,128)(2,1)}, u32[]{:S(2)}) %copy-start.1) | copy-done | bytes 786456
  2.8 0.0 copy-start.2
  2.8 0.9 %copy-done.2 = bf16[1,2,256,256]{3,2,1,0:T(8,128)(2,1)S(1)} copy-done((bf16[1,2,256,256]{3,2,1,0:T(8,128)(2,1)S(1)}, bf16[1,2,256,256]{3,2,1,0:T(8,128)(2,1)}, u32[]{:S(2)}) %copy-start.2) | copy-done | bytes 262168
  3.8 0.0 copy-start.3
  3.8 0.7 copy-done.3
  4.4 63.2 %shard_map.55 = bf16[1,3,2,256,256]{4,3,2,1,0:T(8,128)(2,1)S(1)} custom-call(bf16[3,2,256,256]{3,2,1,0:T(8,128)(2,1)S(1)} %copy-done.1, bf16[2,256,256]{2,1,0:T(8,128)(2,1)S(1)} %bitcast.4, bf16[3,1536,512]{2,1,0:T(8,128)(2,1)} %bitcast.5, bf16[3,1536,256]{2,1,0:T(8,128)(2,1)S(1)} %bitcast.3, f32[1,768]{1,0:T(1,128)S(1)} %copy-done.3), custom_call_target="tpu_custom_call" | custom-call | tf_op jit(solution)/shard_map/pallas_call | solution.py:342
  67.6 0.9 %copy.7 = bf16[1,3,2,256,256]{4,3,2,1,0:T(8,128)(2,1)} copy(bf16[1,3,2,256,256]{4,3,2,1,0:T(8,128)(2,1)S(1)} %shard_map.55) | data formatting | bytes 1572864
Async XLA Ops:
  0.0 1.7 %copy-start = (bf16[1,3,3,512,256]{4,3,2,1,0:T(8,128)(2,1)S(1)}, bf16[1,3,3,512,256]{4,3,2,1,0:T(8,128)(2,1)}, u32[]{:S(2)}) copy-start(bf16[1,3,3,512,256]{4,3,2,1,0:T(8,128)(2,1)} %param.8) | copy-start | bytes 7077892
  1.7 1.1 %copy-start.1 = (bf16[3,2,256,256]{3,2,1,0:T(8,128)(2,1)S(1)}, bf16[3,2,256,256]{3,2,1,0:T(8,128)(2,1)}, u32[]{:S(2)}) copy-start(bf16[3,2,256,256]{3,2,1,0:T(8,128)(2,1)} %frames_ref.1) | copy-start | bytes 2359300
  2.8 0.9 %copy-start.2 = (bf16[1,2,256,256]{3,2,1,0:T(8,128)(2,1)S(1)}, bf16[1,2,256,256]{3,2,1,0:T(8,128)(2,1)}, u32[]{:S(2)}) copy-start(bf16[1,2,256,256]{3,2,1,0:T(8,128)(2,1)} %param.6) | copy-start | bytes 786436
  3.8 0.7 copy-start.3

commit v2 on v1

--- a/solution.py
+++ b/solution.py
@@ -220,26 +220,19 @@
         return im[a * width : a * width + tile, lo : lo + size]
 
     def full(weight, n_lo):
-        total = None
-        for a in range(3):
-            term = jnp.dot(
-                lhs(a, 0, 6 * ch), weight[a, :, n_lo : n_lo + ch],
-                preferred_element_type=jnp.float32,
-            )
-            total = term if total is None else total + term
-        return total
+        return jnp.dot(
+            jnp.concatenate([lhs(a, 0, 6 * ch) for a in range(3)], axis=1),
+            weight[:, :, n_lo : n_lo + ch].reshape(18 * ch, ch),
+            preferred_element_type=jnp.float32,
+        )
 
     def half(weight, base):
-        total = None
-        for a in range(3):
-            for b in range(3):
-                lo = b * 2 * ch + base
-                term = jnp.dot(
-                    lhs(a, lo, ch), weight[a, lo : lo + ch, :],
-                    preferred_element_type=jnp.float32,
-                )
-                total = term if total is None else total + term
-        return total
+        places = [(a, b * 2 * ch + base) for a in range(3) for b in range(3)]
+        return jnp.dot(
+            jnp.concatenate([lhs(a, lo, ch) for a, lo in places], axis=1),
+            jnp.concatenate([weight[a, lo : lo + ch, :] for a, lo in places], axis=0),
+            preferred_element_type=jnp.float32,
+        )
 
     def step(f, carry):
         @pl.when(layer == 0)
@@ -298,6 +291,7 @@
         pl.when(f == 0)(lambda: copy_wc.wait())
         part[...] = half(wc, 0) + bias_ref[:, 2 * ch : 3 * ch]
         exchange(*args, False)
+        pl.when(f > 0)(lambda: send_out(f - 1))
 
         def load_reset(i):
             if i == 0:
@@ -313,12 +307,15 @@
         fresh = (1.0 - update) * hidden + update * candidate
         hs[f + 1] = fresh.astype(jnp.bfloat16).reshape(height, width, ch)
         pl.when(layer < last_layer)(lambda: pass_copy(f).start())
+        return carry
+
+    def send_out(f):
         own_out(f).start()
         for d in range(1, group):
             out_copy(f, d).start()
-        return carry
 
     lax.fori_loop(0, frame_count, step, 0)
+    send_out(frame_count - 1)
 
     def finish(f, carry):
         pl.when(layer < last_layer)(lambda: pass_copy(f).wait_send())
@@ -336,7 +333,7 @@
     height, width = strip * group, cols // group
     dma = pltpu.SemaphoreType.DMA
     bf16, f32 = jnp.bfloat16, jnp.float32
-    anywhere = pl.BlockSpec(memory_space=pl.ANY)
+    anywhere = pl.BlockSpec(memory_space=pltpu.HBM)
     rows_k = w_gates.shape[2] * w_gates.shape[3]
     tile = height * width
     return pl.pallas_call(
@@ -367,7 +364,7 @@
             dma((1, 2)), dma((1, 2)), dma((6,)), dma((6,)),
         ],
         compiler_params=pltpu.CompilerParams(
-            collective_id=0, has_side_effects=True, vmem_limit_bytes=48 * 1024 * 1024
+            collective_id=0, has_side_effects=True, vmem_limit_bytes=66_000_000
         ),
     )(
         frames,

time: 68.7 us -> 64.1 us (0.933)
  local copies, waits for them, and re-layouts: 5.31 us -> 2.06 us
  Pallas kernels: 63.2 us -> 61.8 us
    unnamed x9 -> x1, local copies, waits for them, and re-layouts: 5.31 us -> 2.06 us
    pallas_call x1, Pallas kernels: 63.2 us -> 61.8 us  [shards(): pl.pallas_call(functools.partial(kernel, count, group), out_shape=jax.Sha...]
where the time goes in v2:
time: 64.1 us; the launch traced here: 63.9 us
  Pallas kernels  61.8 us (96%)
  local copies, waits for them, and re-layouts  2.06 us (3%)
    pallas_call x1, Pallas kernels, shards(): pl.pallas_call(functools.partial(kernel, count, group), out_shape=jax.Sha...  61.8 us
    unnamed x1, local copies, waits for them, and re-layouts  2.06 us

profile of v2, /device:TPU:1, one launch (start us, length us, event | category | flops | bytes accessed | tf_op | source)
XLA Modules:
  0.0 63.9 jit_solution(15766542269605039527)
XLA Ops:
  0.0 61.8 %shard_map.55 = bf16[1,3,2,256,256]{4,3,2,1,0:T(8,128)(2,1)} custom-call(bf16[3,2,256,256]{3,2,1,0:T(8,128)(2,1)} %frames_ref.1, bf16[2,256,256]{2,1,0:T(8,128)(2,1)} %bitcast.5, bf16[3,1536,512]{2,1,0:T(8,128)(2,1)} %bitcast.3, bf16[3,1536,256]{2,1,0:T(8,128)(2,1)} %bitcast.4, f32[1,768]{1,0:T(1,128)} %bias_ref.1), custom_call_target="tpu_custom_call" | custom-call | tf_op jit(solution)/shard_map/pallas_call | solution.py:339
  61.9 2.1 %copy.7 = bf16[1,3,2,256,256]{4,3,2,1,0:T(8,128)(2,1)} copy(bf16[1,3,2,256,256]{4,3,2,1,0:T(8,128)(2,1)} %shard_map.55) | data formatting | bytes 1572864

commit v3 on v2

--- a/solution.py
+++ b/solution.py
@@ -110,8 +110,6 @@
             hs.at[f + 1, own_rows], out_ref.at[0, f, :, own_cols, :], out_own.at[f]
         )
 
-    copy_wg.start()
-    copy_wc.start()
     own_init().start()
     pl.when(layer == 0)(lambda: own_frame(0).start())
 
@@ -147,6 +145,8 @@
         for d in range(1, group):
             frame_copy(0, d).start()
 
+    copy_wg.start()
+    copy_wc.start()
     own_init().wait()
     for d in range(1, group):
         init_copy(d).wait()
@@ -364,7 +364,7 @@
             dma((1, 2)), dma((1, 2)), dma((6,)), dma((6,)),
         ],
         compiler_params=pltpu.CompilerParams(
-            collective_id=0, has_side_effects=True, vmem_limit_bytes=66_000_000
+            collective_id=0, has_side_effects=True, vmem_limit_bytes=65_500_000
         ),
     )(
         frames,

time: 64.1 us -> 64.1 us (level)
  no operation moved by 1% of the time
where the time goes in v3:
time: 64.1 us; the launch traced here: 63.9 us
  Pallas kernels  61.8 us (96%)
  local copies, waits for them, and re-layouts  2.06 us (3%)
    pallas_call x1, Pallas kernels, shards(): pl.pallas_call(functools.partial(kernel, count, group), out_shape=jax.Sha...  61.8 us
    unnamed x1, local copies, waits for them, and re-layouts  2.06 us

profile of v3, /device:TPU:1, one launch (start us, length us, event | category | flops | bytes accessed | tf_op | source)
XLA Modules:
  0.0 63.9 jit_solution(4947937905980186014)
XLA Ops:
  0.0 61.8 %shard_map.55 = bf16[1,3,2,256,256]{4,3,2,1,0:T(8,128)(2,1)} custom-call(bf16[3,2,256,256]{3,2,1,0:T(8,128)(2,1)} %frames_ref.1, bf16[2,256,256]{2,1,0:T(8,128)(2,1)} %bitcast.5, bf16[3,1536,512]{2,1,0:T(8,128)(2,1)} %bitcast.3, bf16[3,1536,256]{2,1,0:T(8,128)(2,1)} %bitcast.4, f32[1,768]{1,0:T(1,128)} %bias_ref.1), custom_call_target="tpu_custom_call" | custom-call | tf_op jit(solution)/shard_map/pallas_call | solution.py:339
  61.9 2.1 %copy.7 = bf16[1,3,2,256,256]{4,3,2,1,0:T(8,128)(2,1)} copy(bf16[1,3,2,256,256]{4,3,2,1,0:T(8,128)(2,1)} %shard_map.55) | data formatting | bytes 1572864
